TPU v7x, 256 devices: a whole 4x4x8 slice. The times are simulated.
256 devices in a mesh: azim: 32 (over y_hi, z, core), beam: 2 (over y_lo), sweep: 4 (over x).
Axes of the slice: x: 4, y: 4 (y_hi: 2, y_lo: 2; y = y_hi * 2 + y_lo), z: 8, core: 2. Of those that a mesh axis runs over, the one named last changes fastest.
Arguments:
- features: bfloat16 [2048, 4, 4, 256], P('azim', 'sweep', 'beam'), may hold values from -16 to 16
- cotangent: bfloat16 [2048, 4, 4, 256], P('azim', 'sweep', 'beam'), may hold values from -6 to 6
- w_query: bfloat16 [256, 256], replicated
- w_key: bfloat16 [256, 256], replicated
- w_value: bfloat16 [256, 256], replicated, may hold values from -0.375 to 0.375
- w_out: bfloat16 [256, 256], replicated, may hold values from -0.375 to 0.375
- w_conv: bfloat16 [256, 27, 256], replicated, may hold values from -0.078125 to 0.078125
- sector_mask: int32 [32, 32], replicated, may hold values from 0 to 1, as said below
Outputs:
- features_grad: bfloat16 [2048, 4, 4, 256], P('azim', 'sweep', 'beam')
- weight_grads: float32 [256, 31, 256], P('azim', None, ('beam', 'sweep'))
Inputs may be any that keep to these rules, and one draw needn't show every extreme that they name: `sector_mask`: entry [i, j] is 1 where query sector i may attend to key sector j, else 0; every diagonal entry is 1.
All inputs are finite; a program needn't handle non-finite values.
Results may differ from a plain program's by a relative error of at most 0.012.
The roundings to bfloat16 on the way count: a program that leaves them out, or rounds other values in their place, can miss the bound.
Values may be sent and summed in bfloat16 or wider, within the bound.
A program may use at most 128 MiB of HBM per device.

v0:
```python
import jax
import jax.numpy as jnp
from jax import lax
from jax.sharding import PartitionSpec as P

HEADS = 8
SECTOR = 64
TAPS = 27


highest = lax.Precision.HIGHEST
masked_score = -1e30


def padded_2(block, sides, width):
    for axis, dim in sides:
        count = lax.axis_size(axis)
        forward = [(i, i + 1) for i in range(count - 1)]
        forward.append((count - 1, 0))
        backward = [(target, source) for source, target in forward]
        low = lax.ppermute(
            lax.slice_in_dim(block, block.shape[dim] - width, None, axis=dim), axis, forward
        )
        high = lax.ppermute(lax.slice_in_dim(block, 0, width, axis=dim), axis, backward)
        block = jnp.concatenate([low, block, high], axis=dim)
    return block


def sector_onehot(first_row, row_total, sectors):
    sector_of = (first_row + jnp.arange(row_total, dtype=jnp.int32)) // SECTOR
    return (sector_of[:, None] == jnp.arange(sectors, dtype=jnp.int32)[None, :]).astype(jnp.float32)


def allowed_table(sector_mask, query_first, query_total, key_first, key_total):
    sectors = sector_mask.shape[0]
    query_hot = sector_onehot(query_first, query_total, sectors)
    key_hot = sector_onehot(key_first, key_total, sectors)
    lookup = jnp.dot(jnp.dot(query_hot, sector_mask.astype(jnp.float32)), key_hot.T)
    return lookup > 0.5


def split_heads(tensor):
    return tensor.reshape(tensor.shape[:3] + (HEADS, tensor.shape[3] // HEADS))


def project(flat_rows, weight):
    return jnp.dot(flat_rows, weight, preferred_element_type=jnp.float32).astype(jnp.bfloat16)


def scores_of(queries, key_rows, allowed):
    score_scale = (queries.shape[3] // HEADS) ** (-0.5)
    raw_scores = jnp.einsum(
        "asbhe,ksbhe->sbhak",
        split_heads(queries),
        split_heads(key_rows),
        preferred_element_type=jnp.float32,
    )
    return jnp.where(allowed, raw_scores * score_scale, masked_score)


def key_side(queries, grad_attended, logsum, row_delta, key_rows, value_rows, allowed):
    score_scale = (queries.shape[3] // HEADS) ** (-0.5)
    scores = scores_of(queries, key_rows, allowed)
    weights_full = jnp.where(allowed, jnp.exp(scores - logsum[..., None]), 0.0)
    grad_prob = jnp.einsum(
        "asbhe,ksbhe->sbhak",
        split_heads(grad_attended),
        split_heads(value_rows),
        preferred_element_type=jnp.float32,
    )
    grad_score = (weights_full * (grad_prob - row_delta[..., None])).astype(jnp.bfloat16)
    grad_key = (
        jnp.einsum(
            "sbhak,asbhe->ksbhe",
            grad_score,
            split_heads(queries),
            preferred_element_type=jnp.float32,
        )
        * score_scale
    )
    grad_value = jnp.einsum(
        "sbhak,asbhe->ksbhe",
        weights_full.astype(jnp.bfloat16),
        split_heads(grad_attended),
        preferred_element_type=jnp.float32,
    )
    return (grad_key.reshape(key_rows.shape), grad_value.reshape(key_rows.shape))


def edge_factors(position, devices, length):
    lower_keep = jnp.where(position > 0, 1.0, 0.0).astype(jnp.bfloat16)
    upper_keep = jnp.where(position < devices - 1, 1.0, 0.0).astype(jnp.bfloat16)
    middle = jnp.ones((length,), jnp.bfloat16)
    return jnp.concatenate([lower_keep[None], middle, upper_keep[None]])


def gather_taps(padded, col_count, sweeps, beam_rows, direction):
    pieces = []
    for offset_one in (-1, 0, 1):
        for offset_two in (-1, 0, 1):
            for offset_three in (-1, 0, 1):
                first_at = 1 + direction * offset_one
                second_at = 1 + direction * offset_two
                third_at = 1 + direction * offset_three
                pieces.append(
                    padded[
                        first_at : first_at + col_count,
                        second_at : second_at + sweeps,
                        third_at : third_at + beam_rows,
                    ]
                )
    return jnp.stack(pieces, axis=3)


def per_device(features, cotangent, w_query, w_key, w_value, w_out, w_conv, sector_mask):
    col_count, sweeps, beam_rows, channels = features.shape
    row_count = col_count * sweeps * beam_rows
    flat_in = features.reshape(row_count, channels)
    keep_edges = (
        edge_factors(lax.axis_index("sweep"), lax.axis_size("sweep"), sweeps)[:, None, None]
        * edge_factors(lax.axis_index("beam"), lax.axis_size("beam"), beam_rows)[None, :, None]
    )
    queries = project(flat_in, w_query).reshape(features.shape)
    key_proj = project(flat_in, w_key).reshape(features.shape)
    values = project(flat_in, w_value).reshape(features.shape)
    col_first = lax.axis_index("azim") * col_count
    key_all, value_all = (
        lax.all_gather(key_proj, "azim", axis=0, tiled=True),
        lax.all_gather(values, "azim", axis=0, tiled=True),
    )
    allowed_all = allowed_table(sector_mask, col_first, col_count, 0, key_all.shape[0])
    scores = scores_of(queries, key_all, allowed_all)
    peak_score = jnp.max(scores, axis=-1)
    logsum = peak_score + jnp.log(jnp.sum(jnp.exp(scores - peak_score[..., None]), axis=-1))
    weights_full = jnp.where(allowed_all, jnp.exp(scores - logsum[..., None]), 0.0)
    attended = jnp.einsum(
        "sbhak,ksbhe->asbhe",
        weights_full.astype(jnp.bfloat16),
        split_heads(value_all),
        preferred_element_type=jnp.float32,
    )
    attended = attended.reshape(features.shape).astype(jnp.bfloat16)
    attended_flat = attended.reshape(row_count, channels)
    mixed_out = flat_in.astype(jnp.float32) + jnp.dot(
        attended_flat, w_out, preferred_element_type=jnp.float32
    )
    layer_out = mixed_out.reshape(features.shape).astype(jnp.bfloat16)
    both_pad = (
        padded_2(jnp.stack([layer_out, cotangent]), (("azim", 1), ("beam", 3), ("sweep", 2)), 1)
        * keep_edges
    )
    layer_pad = both_pad[0]
    cot_pad = both_pad[1]
    cot_flat = cotangent.reshape(row_count, channels)
    cot_taps = gather_taps(cot_pad, col_count, sweeps, beam_rows, -1).reshape(
        row_count, TAPS, channels
    )
    grad_layer = cot_flat.astype(jnp.float32) + jnp.einsum(
        "nto,ito->ni", cot_taps, w_conv, preferred_element_type=jnp.float32
    )
    layer_taps = gather_taps(layer_pad, col_count, sweeps, beam_rows, 1).reshape(
        row_count, TAPS, channels
    )
    grad_layer_bf = grad_layer.astype(jnp.bfloat16)
    grad_attended = (
        jnp.dot(grad_layer_bf, w_out.T, preferred_element_type=jnp.float32)
        .astype(jnp.bfloat16)
        .reshape(features.shape)
    )
    row_delta = jnp.einsum(
        "asbhe,asbhe->sbha",
        split_heads(grad_attended),
        split_heads(attended),
        preferred_element_type=jnp.float32,
    )
    grad_prob = jnp.einsum(
        "asbhe,ksbhe->sbhak",
        split_heads(grad_attended),
        split_heads(value_all),
        preferred_element_type=jnp.float32,
    )
    grad_score = (weights_full * (grad_prob - row_delta[..., None])).astype(jnp.bfloat16)
    score_scale = (channels // HEADS) ** (-0.5)
    grad_query = (
        jnp.einsum(
            "sbhak,ksbhe->asbhe",
            grad_score,
            split_heads(key_all),
            preferred_element_type=jnp.float32,
        )
        * score_scale
    )
    grad_query = grad_query.reshape(row_count, channels)
    allowed = allowed_table(
        sector_mask, col_first, col_count, jnp.int32(0), lax.axis_size("azim") * col_count
    )
    grad_key_part, grad_value_part = key_side(
        queries, grad_attended, logsum, row_delta, key_all, value_all, allowed
    )
    key_grads = lax.psum_scatter(
        jnp.concatenate([grad_key_part, grad_value_part], axis=3),
        "azim",
        scatter_dimension=0,
        tiled=True,
    )
    grad_key = key_grads[..., :channels]
    grad_value = key_grads[..., channels:]
    grad_key_flat = grad_key.reshape(row_count, channels)
    grad_value_flat = grad_value.reshape(row_count, channels)
    grad_in = grad_layer + jnp.dot(grad_query, w_query.astype(jnp.float32).T, precision=highest)
    grad_in = grad_in + jnp.dot(grad_key_flat, w_key.astype(jnp.float32).T, precision=highest)
    grad_in = grad_in + jnp.dot(grad_value_flat, w_value.astype(jnp.float32).T, precision=highest)
    features_grad = grad_in.astype(jnp.bfloat16).reshape(features.shape)
    flat_wide = flat_in.astype(jnp.float32)
    projection_terms = jnp.stack(
        [
            jnp.einsum("ni,no->io", flat_wide, grad_query, precision=highest),
            jnp.einsum("ni,no->io", flat_wide, grad_key_flat, precision=highest),
            jnp.einsum("ni,no->io", flat_wide, grad_value_flat, precision=highest),
            jnp.einsum(
                "ni,no->io", attended_flat, grad_layer_bf, preferred_element_type=jnp.float32
            ),
        ],
        axis=1,
    )
    conv_terms = jnp.einsum("nti,no->ito", layer_taps, cot_flat, preferred_element_type=jnp.float32)
    weight_rows = lax.psum_scatter(
        jnp.concatenate([projection_terms, conv_terms], axis=1),
        "azim",
        scatter_dimension=0,
        tiled=True,
    )
    weight_grads = lax.psum_scatter(weight_rows, ("beam", "sweep"), scatter_dimension=2, tiled=True)
    return (features_grad, weight_grads)


def solution(mesh):
    in_specs = (
        P("azim", "sweep", "beam", None),
        P("azim", "sweep", "beam", None),
        P(),
        P(),
        P(),
        P(),
        P(),
        P(),
    )
    out_specs = (P("azim", "sweep", "beam", None), P("azim", None, ("beam", "sweep")))
    return jax.shard_map(
        per_device, mesh=mesh, in_specs=in_specs, out_specs=out_specs, check_vma=False
    )
```

profile of v0, /device:TPU:1, one launch (start us, length us, event | category | flops | bytes accessed | tf_op | source)
XLA Modules:
  0.0 746.9 jit_solution(16207301087636658915)
XLA Ops:
  22.3 2.0 convolution_compare_fusion
  24.3 72.0 %all-gather.5.cloned.1.call-done = bf16[2048,1,2,256]{3,2,1,0:T(2,128)(2,1)} async-done(((bf16[64,1,2,256]{3,2,1,0:T(2,128)(2,1)}), bf16[2048,1,2,256]{3,2,1,0:T(2,128)(2,1)}) %all-gather.5.cloned.1.call-update) | async-done | bytes 2097168 | tf_op jit(solution)/shard_map/all_gather | solution.py:128
  96.3 6.2 copy.105
  102.5 3.5 fusion.1
  106.0 2.2 exponential_reduce_fusion
  109.2 66.8 %all-gather.3.cloned.1.call-done = bf16[2048,1,2,256]{3,2,1,0:T(2,128)(2,1)} async-done(((bf16[64,1,2,256]{3,2,1,0:T(2,128)(2,1)}), bf16[2048,1,2,256]{3,2,1,0:T(2,128)(2,1)}) %all-gather.3.cloned.1.call-update) | async-done | bytes 2097168 | tf_op jit(solution)/shard_map/all_gather | solution.py:129
  176.0 6.2 copy.103
  182.2 6.8 convolution_convert_fusion
  208.7 2.4 collective-permute-start.5
  215.1 3.1 collective-permute-done.4
  333.0 2.8 fusion.5
  337.4 8.2 %fusion.28 = f32[2,8,32,2048]{3,2,1,0:T(8,128)} fusion(bf16[64,2,8,32]{0,3,2,1:T(8,128)(2,1)S(1)} %copy.137, f32[2,8,64,2048]{3,2,1,0:T(8,128)} %copy-done.2, f32[2,8,64]{2,1,0:T(8,128)S(1)} %log_add_fusion, pred[64,2048]{1,0:T(8,128)(4,1)S(1)} %copy-done.12), kind=kOutput, calls=%fused_computation.156 | convolution fusion | flops 144703488 | bytes 12783616 | tf_op jit(solution)/shard_map/sbhak,asbhe->ksbhe/dot_general | solution.py:81
  345.7 7.2 multiply_convert_fusion
  352.8 5.4 copy.142
  358.2 5.0 convolution_multiply_fusion
  363.2 5.4 copy.141
  368.6 7.9 %pad_maximum_fusion = f32[2048,1,2,512]{3,0,2,1:T(8,128)} fusion(f32[2048,1,2,256]{3,0,2,1:T(8,128)} %copy.142, f32[2048,1,2,256]{3,0,2,1:T(8,128)} %copy.141), kind=kLoop, calls=%fused_computation | loop fusion | flops 2097152 | bytes 16777216 | tf_op jit(solution)/shard_map/concatenate | solution.py:201
  378.1 3.4 fusion.3
  383.8 144.8 %reduce-scatter.6.cloned.1.call-done = f32[64,1,2,512]{3,0,2,1:T(8,128)} async-done(((f32[2048,1,2,512]{3,0,2,1:T(8,128)}), f32[64,1,2,512]{3,0,2,1:T(8,128)}) %reduce-scatter.6.cloned.1.call-update) | async-done | bytes 262160 | tf_op jit(solution)/shard_map/reduce_scatter | solution.py:200
  533.7 3.9 bitcast_dynamic-update-slice_fusion
  539.6 150.0 %reduce-scatter.8.cloned.1.call-done = f32[8,31,256]{2,0,1:T(8,128)} async-done(((f32[256,31,256]{2,0,1:T(8,128)}), f32[8,31,256]{2,0,1:T(8,128)}) %reduce-scatter.8.cloned.1.call-update) | async-done | bytes 253968 | tf_op jit(solution)/shard_map/reduce_scatter | solution.py:227
  689.6 5.2 copy.159
  694.8 4.6 reshape.318
  711.7 24.9 %reduce-scatter.10.cloned.1.call-done = f32[32,248]{1,0:T(8,128)} async-done(((f32[256,248]{1,0:T(8,128)}), f32[32,248]{1,0:T(8,128)}) %reduce-scatter.10.cloned.1.call-update) | async-done | bytes 31760
  (255 shorter events, 182.7 us)
Async XLA Ops:
  7.2 325.8 %copy-start = (bf16[256,27,256]{2,0,1:T(8,128)(2,1)S(1)}, bf16[256,27,256]{2,0,1:T(8,128)(2,1)}, u32[]{:S(2)}) copy-start(bf16[256,27,256]{2,0,1:T(8,128)(2,1)} %param.14) | copy-start | bytes 10616836
  7.2 89.1 %all-gather.5.cloned.1.call-start = ((), (), s32[]{:S(2)}) async-start(), calls=%async_computation.4 | async-start | bytes 2162688 | tf_op jit(solution)/shard_map/all_gather | solution.py:128
  12.1 163.9 %all-gather.3.cloned.1.call-start = ((), (), s32[]{:S(2)}) async-start(), calls=%async_computation.3 | async-start | bytes 2162688 | tf_op jit(solution)/shard_map/all_gather | solution.py:129
  15.4 513.2 %reduce-scatter.6.cloned.1.call-start = ((), (), s32[]{:S(2)}) async-start(), calls=%async_computation.5 | async-start | bytes 8650752 | tf_op jit(solution)/shard_map/reduce_scatter | solution.py:200
  198.6 3.2 collective-permute-start.1
  198.9 3.0 collective-permute-start
  202.8 3.6 collective-permute-start.3
  203.6 3.4 collective-permute-start.2
  208.7 6.4 collective-permute-start.5
  211.1 7.1 collective-permute-start.4
  304.5 24.6 %copy-start.28 = (bf16[128,1,256]{2,0,1:T(8,128)(2,1)S(1)}, bf16[128,1,256]{2,0,1:T(8,128)(2,1)}, u32[]{:S(2)}) copy-start(bf16[128,1,256]{2,0,1:T(8,128)(2,1)} %stack.210) | copy-start | bytes 196612
  304.6 25.2 %copy-start.29 = (bf16[128,1,256]{2,0,1:T(8,128)(2,1)S(1)}, bf16[128,1,256]{2,0,1:T(8,128)(2,1)}, u32[]{:S(2)}) copy-start(bf16[128,1,256]{2,0,1:T(8,128)(2,1)} %stack.211) | copy-start | bytes 196612
  304.6 25.9 %copy-start.30 = (bf16[128,1,256]{2,0,1:T(8,128)(2,1)S(1)}, bf16[128,1,256]{2,0,1:T(8,128)(2,1)}, u32[]{:S(2)}) copy-start(bf16[128,1,256]{2,0,1:T(8,128)(2,1)} %stack.212) | copy-start | bytes 196612
  304.6 26.5 %copy-start.31 = (bf16[128,1,256]{2,0,1:T(8,128)(2,1)S(1)}, bf16[128,1,256]{2,0,1:T(8,128)(2,1)}, u32[]{:S(2)}) copy-start(bf16[128,1,256]{2,0,1:T(8,128)(2,1)} %stack.213) | copy-start | bytes 196612
  304.6 27.1 %copy-start.32 = (bf16[128,1,256]{2,0,1:T(8,128)(2,1)S(1)}, bf16[128,1,256]{2,0,1:T(8,128)(2,1)}, u32[]{:S(2)}) copy-start(bf16[128,1,256]{2,0,1:T(8,128)(2,1)} %stack.214) | copy-start | bytes 196612
  304.6 27.7 %copy-start.33 = (bf16[128,1,256]{2,0,1:T(8,128)(2,1)S(1)}, bf16[128,1,256]{2,0,1:T(8,128)(2,1)}, u32[]{:S(2)}) copy-start(bf16[128,1,256]{2,0,1:T(8,128)(2,1)} %stack.215) | copy-start | bytes 196612
  304.6 28.4 %copy-start.17 = (f32[128,256]{1,0:T(8,128)S(1)}, f32[128,256]{1,0:T(8,128)}, u32[]{:S(2)}) copy-start(f32[128,256]{1,0:T(8,128)} %reshape.309) | copy-start | bytes 393220
  376.5 313.0 %reduce-scatter.8.cloned.1.call-start = ((), (), s32[]{:S(2)}) async-start(), calls=%async_computation.6 | async-start | bytes 8380416 | tf_op jit(solution)/shard_map/reduce_scatter | solution.py:227
  383.2 145.4 %copy-start.15 = (bf16[64,1,2,256]{3,2,1,0:T(2,128)(2,1)S(1)}, bf16[64,1,2,256]{3,2,1,0:T(2,128)(2,1)}, u32[]{:S(2)}) copy-start(bf16[64,1,2,256]{3,2,1,0:T(2,128)(2,1)} %param.8) | copy-start | bytes 196612
  383.7 149.1 %copy-start.7 = (f32[128,256]{1,0:T(8,128)S(1)}, f32[128,256]{1,0:T(8,128)}, u32[]{:S(2)}) copy-start(f32[128,256]{1,0:T(8,128)} %copy-done.6) | copy-start | bytes 393220
  383.7 149.1 %copy-start.14 = (bf16[128,256]{1,0:T(8,128)(2,1)S(1)}, bf16[128,256]{1,0:T(8,128)(2,1)}, u32[]{:S(2)}) copy-start(bf16[128,256]{1,0:T(8,128)(2,1)} %convert_element_type.105) | copy-start | bytes 196612
  383.8 149.9 %copy-start.13 = (bf16[64,1,2,256]{3,2,1,0:T(2,128)(2,1)S(1)}, bf16[64,1,2,256]{3,2,1,0:T(2,128)(2,1)}, u32[]{:S(2)}) copy-start(bf16[64,1,2,256]{3,2,1,0:T(2,128)(2,1)} %param.9) | copy-start | bytes 196612
  537.7 198.9 %reduce-scatter.10.cloned.1.call-start = ((), (), s32[]{:S(2)}) async-start(), calls=%async_computation.7 | async-start | bytes 294912
  699.4 41.0 %copy-start.1 = (bf16[256,27,256]{2,0,1:T(8,128)(2,1)S(1)}, bf16[256,27,256]{2,0,1:T(8,128)(2,1)}, u32[]{:S(2)}) copy-start(bf16[256,27,256]{2,0,1:T(8,128)(2,1)} %param.14) | copy-start | bytes 10616836
  (21 other events, 173.4 us)
Sparse Core Ops, SparseCore 0:
  12.2 84.0 all-gather.4
  99.6 76.3 all-gather.2
  376.6 151.9 reduce-scatter.5
  537.8 151.7 reduce-scatter.7
  699.5 36.9 reduce-scatter.9
where the time goes:
time: 756 us; the launch traced here: 747 us
  waiting for transfers between devices  466 us (62%)
  local copies, waits for them, and re-layouts  185 us (24%)
  matrix products  57.8 us (8%)
  other arithmetic  17.5 us (2%)
  between operations  14.4 us (2%)
    reduce_scatter x1, waiting for transfers between devices, per_device(): lax.psum_scatter(jnp.concatenate([projection_terms, conv_terms], axis=1),...  150 us
    reduce_scatter x1, waiting for transfers between devices, per_device(): lax.psum_scatter(jnp.concatenate([grad_key_part, grad_value_part], axis=3...  145 us
    all_gather x1, waiting for transfers between devices, per_device(): lax.all_gather(key_proj, 'azim', axis=0, tiled=True)  72 us
    all_gather x1, waiting for transfers between devices, per_device(): lax.all_gather(values, 'azim', axis=0, tiled=True)  66.8 us
    unnamed x129, local copies, waits for them, and re-layouts  51.9 us
    slice x29, local copies, waits for them, and re-layouts, gather_taps(): padded[first_at:first_at + col_count, second_at:second_at + sweeps, third...  42.1 us
    another operation x29, local copies, waits for them, and re-layouts, gather_taps(): return jnp.stack(pieces, axis=3)  41 us
    unnamed x6, waiting for transfers between devices  25 us
  transfers between devices with their start and end apart: 11, of which 10 were waited for; matrix products, arithmetic and copies ran while one was open for 6% of the time, Pallas kernels for 0%

commit v1 on v0

v1 whole, which is shorter than its diff:
```python
import functools

import jax
import jax.numpy as jnp
from jax import lax
from jax.experimental import pallas as pl
from jax.experimental.pallas import tpu as pltpu
from jax.sharding import PartitionSpec as P

HEADS = 8
HEAD = 32
COLS = 64
RING = 32
CHIPS = 16
GROUP = 8
SWEEPS = 4
TAPS = 27
TILE = 256
SCALE = HEAD ** (-0.5)
MASKED = -1e30
MESH = pl.DeviceIdType.MESH
VMEM = pl.BlockSpec(memory_space=pltpu.VMEM)
F32 = jnp.float32
BF16 = jnp.bfloat16


def place():
    return lax.axis_index("azim"), lax.axis_index("beam"), lax.axis_index("sweep")


def member(azim, index):
    return (azim, lax.div(index, SWEEPS), lax.rem(index, SWEEPS))


def greet(devices):
    barrier = pltpu.get_barrier_semaphore()
    total = 0
    for first, last, device in devices:

        def one(i, carry, device=device):
            pl.semaphore_signal(barrier, inc=1, device_id=device(i), device_id_type=MESH)
            return carry

        lax.fori_loop(first, last, one, 0)
        total += last - first
    pl.semaphore_wait(barrier, total)


def remote(src, dst, send, recv, device):
    return pltpu.make_async_remote_copy(
        src_ref=src, dst_ref=dst, send_sem=send, recv_sem=recv, device_id=device, device_id_type=MESH
    )


def each(first, last, action):
    def step(i, carry):
        action(i)
        return carry

    lax.fori_loop(first, last, step, 0)


def halo_kernel(cot, edges, cot_all, low, high, send, recv, send_low, recv_low, send_high, recv_high):
    azim, beam, sweep = place()
    me = beam * SWEEPS + sweep
    after = lax.rem(azim + 1, RING)
    before = lax.rem(azim + RING - 1, RING)
    peer = lambda i: lax.rem(me + i, GROUP)
    greet(
        [
            (1, GROUP, lambda i: member(azim, peer(i))),
            (0, GROUP, lambda i: member(after, i)),
            (0, GROUP, lambda i: member(before, i)),
        ]
    )
    each(
        0,
        GROUP,
        lambda i: remote(
            edges.at[1], low.at[me], send_low.at[i], recv_low.at[me], member(after, i)
        ).start(),
    )
    each(
        0,
        GROUP,
        lambda i: remote(
            edges.at[0], high.at[me], send_high.at[i], recv_high.at[me], member(before, i)
        ).start(),
    )
    each(
        1,
        GROUP,
        lambda i: remote(
            cot, cot_all.at[me], send.at[peer(i)], recv.at[me], member(azim, peer(i))
        ).start(),
    )
    cot_all[pl.ds(me, 1)] = cot[...][None]
    each(
        1,
        GROUP,
        lambda i: remote(
            cot, cot_all.at[peer(i)], send.at[peer(i)], recv.at[peer(i)], member(azim, peer(i))
        ).wait(),
    )
    each(
        0,
        GROUP,
        lambda i: remote(
            edges.at[1], low.at[i], send_low.at[i], recv_low.at[i], member(after, i)
        ).wait(),
    )
    each(
        0,
        GROUP,
        lambda i: remote(
            edges.at[0], high.at[i], send_high.at[i], recv_high.at[i], member(before, i)
        ).wait(),
    )


def shifted(block, low, high):
    rows = lax.broadcasted_iota(jnp.int32, block.shape, 0)
    down = jnp.where(rows == 0, low, pltpu.roll(block, 1, 0))
    up = jnp.where(rows == COLS - 1, high, pltpu.roll(block, COLS - 1, 0))
    return up, block, down


def regroup():
    col = lax.broadcasted_iota(jnp.int32, (1, 1024), 1)
    source = ((col >> 5) & 3) * 256 + (col >> 7) * 32 + (col & 31)
    row = lax.broadcasted_iota(jnp.int32, (1024, 1024), 0)
    return jnp.where(row == source, 1.0, 0.0).astype(BF16)


def dot(left, right):
    return jnp.dot(left, right, preferred_element_type=F32)


def dot_nt(left, right):
    return lax.dot_general(left, right, (((1,), (1,)), ((), ())), preferred_element_type=F32)


def project_kernel(cot_all, low, high, feat, w_query, w_key, w_value, w_out, w_conv, grad_out, pack):
    _, beam, sweep = place()
    total = jnp.zeros((2 * COLS, 256), F32)
    for j in (-1, 0, 1):
        for k in (-1, 0, 1):
            ups, mids, downs = [], [], []
            for own in (0, 1):
                s_at = sweep - j
                b_at = beam * 2 + own - k
                inside = (s_at >= 0) & (s_at < SWEEPS) & (b_at >= 0) & (b_at < 4)
                s_at = jnp.clip(s_at, 0, SWEEPS - 1)
                pair_at = jnp.clip(beam + (own - k) // 2, 0, 1)
                index = pair_at * SWEEPS + s_at
                half = (own - k) % 2
                keep = jnp.where(inside, 1.0, 0.0)
                block = cot_all[index, half].astype(F32) * keep
                up, mid, down = shifted(
                    block,
                    low[index].astype(F32)[half : half + 1] * keep,
                    high[index].astype(F32)[half : half + 1] * keep,
                )
                ups.append(up)
                mids.append(mid)
                downs.append(down)
            for i, rows in ((-1, ups), (0, mids), (1, downs)):
                tap = 9 * (i + 1) + 3 * (j + 1) + (k + 1)
                rows = jnp.concatenate(rows, axis=0).astype(BF16)
                total += dot_nt(rows, w_conv[tap])
    me = beam * SWEEPS + sweep
    grad = cot_all[me].astype(F32).reshape(2 * COLS, 256) + total
    grad_out[...] = grad
    grad_att = dot_nt(grad.astype(BF16), w_out[...]).astype(BF16)
    rows = feat[...]
    queries = dot(rows, w_query[...]).astype(BF16)
    keys = dot(rows, w_key[...]).astype(BF16)
    values = dot(rows, w_value[...]).astype(BF16)
    wide = jnp.concatenate([keys, queries, grad_att, values], axis=1)
    packed = dot(wide, regroup()).astype(BF16)
    for b in (0, 1):
        for h in range(HEADS):
            pack[b * HEADS + h] = packed[b * COLS : (b + 1) * COLS, h * 128 : (h + 1) * 128]


def spread_kernel(pack, feat, same, other, feat_all, send, recv, send_f, recv_f, own_sem, pair_sem):
    azim, beam, sweep = place()
    me = beam * SWEEPS + sweep
    chip = lax.div(azim, 2)
    core = lax.rem(azim, 2)
    sibling = (2 * chip + 1 - core, beam, sweep)
    target = lambda i: lax.rem(chip + i, CHIPS)
    device = lambda q: (2 * q + core, beam, sweep)
    peer = lambda i: lax.rem(me + i, GROUP)
    greet(
        [
            (1, CHIPS, lambda i: device(target(i))),
            (0, 1, lambda i: sibling),
            (1, GROUP, lambda i: member(azim, peer(i))),
        ]
    )
    keep = pltpu.make_async_copy(pack.at[chip], same.at[chip], own_sem)
    keep.start()
    each(
        1,
        CHIPS,
        lambda i: remote(
            pack.at[target(i)], same.at[chip], send.at[target(i)], recv.at[chip], device(target(i))
        ).start(),
    )
    each(
        1,
        GROUP,
        lambda i: remote(
            feat, feat_all.at[me], send_f.at[peer(i)], recv_f.at[me], member(azim, peer(i))
        ).start(),
    )
    feat_all[pl.ds(me, 1)] = feat[...][None]
    keep.wait()
    each(
        1,
        CHIPS,
        lambda i: remote(
            pack.at[target(i)],
            same.at[target(i)],
            send.at[target(i)],
            recv.at[target(i)],
            device(target(i)),
        ).wait(),
    )
    relay = remote(same, other, pair_sem.at[0], pair_sem.at[1], sibling)
    relay.start()
    each(
        1,
        GROUP,
        lambda i: remote(
            feat, feat_all.at[peer(i)], send_f.at[peer(i)], recv_f.at[peer(i)], member(azim, peer(i))
        ).wait(),
    )
    relay.wait()


def attention_kernel(same, other, mask, out_same, out_other, rows_all, cols_all, cols_own, allowed, back, keys_sum):
    core = lax.rem(lax.axis_index("azim"), 2)
    sub = lax.broadcasted_iota(jnp.int32, (32, 32), 0)
    lane = lax.broadcasted_iota(jnp.int32, (32, 32), 1)
    key_sector = jnp.where(sub < CHIPS, 2 * sub + core, 2 * (sub - CHIPS) + 1 - core)
    key_hot = jnp.where(lane == key_sector, 1.0, 0.0).astype(BF16)
    by_query = dot_nt(key_hot, mask[...].astype(F32).astype(BF16)).astype(BF16)
    lane = lax.broadcasted_iota(jnp.int32, (32, 1024), 1)
    sub = lax.broadcasted_iota(jnp.int32, (32, 1024), 0)
    query_hot = jnp.where(sub == 2 * (lane >> 6) + core, 1.0, 0.0).astype(BF16)
    full = dot(by_query, query_hot)
    rows_all[0:1024] = same[...]
    rows_all[1024:2048] = other[...]
    own_t = same[...].astype(F32).T.astype(BF16)
    cols_all[:, 0:1024] = own_t
    cols_all[:, 1024:2048] = other[...].astype(F32).T.astype(BF16)
    for t in range(1024 // TILE):
        cols_own[t] = own_t[:, t * TILE : (t + 1) * TILE]
        allowed[t] = full[:, t * TILE : (t + 1) * TILE]
    keys_sum[...] = jnp.zeros_like(keys_sum)

    def tile(t, carry):
        cols = cols_own[t]
        rows = same[pl.ds(pl.multiple_of(t * TILE, TILE), TILE), :]
        keep = allowed[t][:, None, :]
        blank = jnp.zeros((96, TILE), BF16)
        score = dot(rows_all[...], jnp.concatenate([cols[32:64], blank], axis=0))
        score = score.reshape(32, COLS, TILE) * SCALE
        score = jnp.where(keep > 0.5, score, MASKED)
        peak = jnp.max(jnp.max(score, axis=0), axis=0, keepdims=True)
        weight = jnp.exp(score - peak[None])
        total = jnp.sum(jnp.sum(weight, axis=0), axis=0, keepdims=True)
        weight = weight * (keep * (1.0 / total)[None])
        probs = weight.reshape(2048, TILE).astype(BF16)
        attended = dot(cols_all[96:128, :], probs).astype(BF16)
        grad_att = cols[64:96]
        delta = jnp.sum(grad_att.astype(F32) * attended.astype(F32), axis=0, keepdims=True)
        grad_prob = dot(rows_all[...], jnp.concatenate([blank, grad_att], axis=0))
        grad_score = weight * (grad_prob.reshape(32, COLS, TILE) - delta[None])
        grad_score = grad_score.reshape(2048, TILE).astype(BF16)
        grad_query = dot(cols_all[0:32, :], grad_score) * SCALE
        place_at = lax.broadcasted_iota(jnp.int32, (TILE, 128), 1) >> 5
        zero = jnp.zeros((TILE, 128), BF16)
        keys_sum[...] += dot(grad_score, jnp.where(place_at == 1, rows, zero)) * SCALE + dot(
            probs, jnp.where(place_at == 2, rows, zero)
        )
        joined = jnp.concatenate(
            [grad_query, jnp.zeros((64, TILE), F32), attended.astype(F32)], axis=0
        )
        back[pl.ds(pl.multiple_of(t * TILE, TILE), TILE), :] = joined.T
        return carry

    lax.fori_loop(0, 1024 // TILE, tile, 0)
    out_same[...] = (keys_sum[0:1024] + back[...]).astype(BF16)
    out_other[...] = keys_sum[1024:2048].astype(BF16)


def return_kernel(out_same, out_other, from_same, from_other, send, recv, send_o, recv_o, own_sem):
    azim, beam, sweep = place()
    chip = lax.div(azim, 2)
    core = lax.rem(azim, 2)
    target = lambda i: lax.rem(chip + i, CHIPS)
    like = lambda q: (2 * q + core, beam, sweep)
    unlike = lambda q: (2 * q + 1 - core, beam, sweep)
    greet(
        [
            (1, CHIPS, lambda i: like(target(i))),
            (0, CHIPS, lambda i: unlike(target(i))),
        ]
    )
    keep = pltpu.make_async_copy(out_same.at[chip], from_same.at[chip], own_sem)
    keep.start()
    each(
        1,
        CHIPS,
        lambda i: remote(
            out_same.at[target(i)],
            from_same.at[chip],
            send.at[target(i)],
            recv.at[chip],
            like(target(i)),
        ).start(),
    )
    each(
        0,
        CHIPS,
        lambda i: remote(
            out_other.at[target(i)],
            from_other.at[chip],
            send_o.at[target(i)],
            recv_o.at[chip],
            unlike(target(i)),
        ).start(),
    )
    keep.wait()
    each(
        1,
        CHIPS,
        lambda i: remote(
            out_same.at[target(i)],
            from_same.at[target(i)],
            send.at[target(i)],
            recv.at[target(i)],
            like(target(i)),
        ).wait(),
    )
    each(
        0,
        CHIPS,
        lambda i: remote(
            out_other.at[target(i)],
            from_other.at[target(i)],
            send_o.at[target(i)],
            recv_o.at[target(i)],
            unlike(target(i)),
        ).wait(),
    )


def collect_kernel(from_same, from_other, grad, w_query, w_key, w_value, feat_grad, att_out, blocks):
    summed = []
    for b in (0, 1):
        heads = [
            (from_same[b * HEADS + h].astype(F32) + from_other[b * HEADS + h].astype(F32)).astype(BF16)
            for h in range(HEADS)
        ]
        summed.append(jnp.concatenate(heads, axis=1))
    packed = jnp.concatenate(summed, axis=0)
    order = regroup()
    wide = dot_nt(packed, order).astype(BF16)
    grad_f = grad[...]
    feat_grad[...] = (
        grad_f
        + dot_nt(wide[:, 0:256], w_query[...])
        + dot_nt(wide[:, 256:512], w_key[...])
        + dot_nt(wide[:, 512:768], w_value[...])
    ).astype(BF16)
    att_out[...] = wide[:, 768:1024]
    last = dot(grad_f.astype(BF16), order[768:1024, :])
    group = (lax.broadcasted_iota(jnp.int32, (2 * COLS, 1024), 1) >> 5) & 3
    merged = jnp.where(group == 3, last, packed.astype(F32)).astype(BF16)
    for h in range(HEADS):
        blocks[h] = merged[:, h * 128 : (h + 1) * 128]


def share_kernel(att, blocks, att_all, block_all, send, recv, send_b, recv_b):
    azim, beam, sweep = place()
    me = beam * SWEEPS + sweep
    peer = lambda i: lax.rem(me + i, GROUP)
    greet([(1, GROUP, lambda i: member(azim, peer(i)))])
    each(
        1,
        GROUP,
        lambda i: remote(
            att, att_all.at[me], send.at[peer(i)], recv.at[me], member(azim, peer(i))
        ).start(),
    )
    each(
        1,
        GROUP,
        lambda i: remote(
            blocks.at[peer(i)],
            block_all.at[me],
            send_b.at[peer(i)],
            recv_b.at[me],
            member(azim, peer(i)),
        ).start(),
    )
    att_all[pl.ds(me, 1)] = att[...][None]
    block_all[pl.ds(me, 1)] = blocks[pl.ds(me, 1)]
    each(
        1,
        GROUP,
        lambda i: remote(
            att, att_all.at[peer(i)], send.at[peer(i)], recv.at[peer(i)], member(azim, peer(i))
        ).wait(),
    )
    each(
        1,
        GROUP,
        lambda i: remote(
            blocks.at[peer(i)],
            block_all.at[peer(i)],
            send_b.at[peer(i)],
            recv_b.at[peer(i)],
            member(azim, peer(i)),
        ).wait(),
    )


def weight_kernel(cot_all, low, high, feat_all, att_all, block_all, w_out, part, taps):
    _, beam, sweep = place()
    me = beam * SWEEPS + sweep
    row = lax.broadcasted_iota(jnp.int32, (256, 128), 0)
    col = lax.broadcasted_iota(jnp.int32, (256, 128), 1)
    pick = jnp.where(row == me * HEAD + (col & 31), 1.0, 0.0).astype(BF16)
    own = dot(cot_all[...].reshape(1024, 256), pick)
    own_low = dot(low[...], pick)
    own_high = dot(high[...], pick)
    moved = []
    for n in range(16):
        moved.append(
            shifted(
                own[n * COLS : (n + 1) * COLS], own_low[n : n + 1], own_high[n : n + 1]
            )
        )
    lane = lax.broadcasted_iota(jnp.int32, (COLS, 128), 1) >> 5
    zero = jnp.zeros((COLS, 128), F32)

    def find(n, tap):
        if tap >= TAPS:
            return zero
        i, j, k = tap // 9, tap // 3 % 3 - 1, tap % 3 - 1
        s = (n // 2) % SWEEPS - j
        b = (n // 2) // SWEEPS * 2 + n % 2 - k
        if not (0 <= s < SWEEPS and 0 <= b < 4):
            return zero
        return moved[(b // 2 * SWEEPS + s) * 2 + b % 2][i]

    for g in range(7):
        for n in range(16):
            value = find(n, 4 * g)
            for r in (1, 2, 3):
                value = jnp.where(lane == r, find(n, 4 * g + r), value)
            taps[n * COLS : (n + 1) * COLS, g * 128 : (g + 1) * 128] = value.astype(BF16)
    feats = feat_all[...].reshape(1024, 256)
    atts = att_all[...].reshape(1024, 256)
    layer = (feats.astype(F32) + dot(atts, w_out[...])).astype(BF16)
    blocks = block_all[...].reshape(1024, 128)
    first = dot(feats.astype(F32).T.astype(BF16), blocks)
    fourth = dot(atts.astype(F32).T.astype(BF16), blocks)
    col = lax.broadcasted_iota(jnp.int32, (256, 128), 1) >> 5
    part[:, :, 0:128] = jnp.where(col == 3, fourth, first).reshape(RING, 8, 128)
    part[:, :, 128:1024] = dot(layer.astype(F32).T.astype(BF16), taps[...]).reshape(RING, 8, 896)


def reduce_kernel(part, total, landed, send, recv):
    azim, beam, sweep = place()
    target = lambda i: lax.rem(azim + i, RING)
    device = lambda q: (q, beam, sweep)
    greet([(1, RING, lambda i: device(target(i)))])
    each(
        1,
        RING,
        lambda i: remote(
            part.at[target(i)], landed.at[azim], send.at[target(i)], recv.at[azim], device(target(i))
        ).start(),
    )
    total[...] = part[azim].astype(F32)

    def add(i):
        remote(
            part.at[target(i)],
            landed.at[target(i)],
            send.at[target(i)],
            recv.at[target(i)],
            device(target(i)),
        ).wait()
        total[...] += landed[target(i)].astype(F32)

    each(1, RING, add)


def shape(dims, kind=BF16):
    return jax.ShapeDtypeStruct(dims, kind)


def call(kernel, inputs, outputs, scratch, collective=None):
    remote_call = collective is not None
    return pl.pallas_call(
        kernel,
        out_shape=outputs,
        in_specs=[VMEM] * len(inputs),
        out_specs=jax.tree.map(lambda _: VMEM, outputs),
        scratch_shapes=scratch,
        compiler_params=pltpu.CompilerParams(
            collective_id=collective,
            has_side_effects=remote_call,
            vmem_limit_bytes=60 * 1024 * 1024,
        ),
    )(*inputs)


def dma(*dims):
    return pltpu.SemaphoreType.DMA(dims)


def per_device(features, cotangent, w_query, w_key, w_value, w_out, w_conv, sector_mask):
    feat = features.reshape(COLS, 2, 256).transpose(1, 0, 2)
    cot = cotangent.reshape(COLS, 2, 256).transpose(1, 0, 2)
    edges = jnp.stack([cotangent[0, 0], cotangent[COLS - 1, 0]])
    conv = w_conv.transpose(1, 0, 2)
    feat = feat.reshape(2 * COLS, 256)
    cot_all, low, high = call(
        halo_kernel,
        (cot, edges),
        (shape((GROUP, 2, COLS, 256)), shape((GROUP, 2, 256)), shape((GROUP, 2, 256))),
        [dma(GROUP) for _ in range(6)],
        1,
    )
    grad, pack = call(
        project_kernel,
        (cot_all, low, high, feat, w_query, w_key, w_value, w_out, conv),
        (shape((2 * COLS, 256), F32), shape((CHIPS, COLS, 128))),
        [],
    )
    same, other, feat_all = call(
        spread_kernel,
        (pack, feat),
        (shape((CHIPS, COLS, 128)), shape((CHIPS, COLS, 128)), shape((GROUP, 2 * COLS, 256))),
        [dma(CHIPS), dma(CHIPS), dma(GROUP), dma(GROUP), pltpu.SemaphoreType.DMA, dma(2)],
        2,
    )
    out_same, out_other = call(
        attention_kernel,
        (same.reshape(1024, 128), other.reshape(1024, 128), sector_mask),
        (shape((1024, 128)), shape((1024, 128))),
        [
            pltpu.VMEM((2048, 128), BF16),
            pltpu.VMEM((128, 2048), BF16),
            pltpu.VMEM((1024 // TILE, 128, TILE), BF16),
            pltpu.VMEM((1024 // TILE, 32, TILE), F32),
            pltpu.VMEM((1024, 128), F32),
            pltpu.VMEM((2048, 128), F32),
        ],
    )
    from_same, from_other = call(
        return_kernel,
        (out_same.reshape(CHIPS, COLS, 128), out_other.reshape(CHIPS, COLS, 128)),
        (shape((CHIPS, COLS, 128)), shape((CHIPS, COLS, 128))),
        [dma(CHIPS), dma(CHIPS), dma(CHIPS), dma(CHIPS), pltpu.SemaphoreType.DMA],
        3,
    )
    feat_grad, att, blocks = call(
        collect_kernel,
        (from_same, from_other, grad, w_query, w_key, w_value),
        (shape((2 * COLS, 256)), shape((2 * COLS, 256)), shape((HEADS, 2 * COLS, 128))),
        [],
    )
    att_all, block_all = call(
        share_kernel,
        (att, blocks),
        (shape((GROUP, 2 * COLS, 256)), shape((GROUP, 2 * COLS, 128))),
        [dma(GROUP) for _ in range(4)],
        4,
    )
    part = call(
        weight_kernel,
        (
            cot_all,
            low.reshape(16, 256),
            high.reshape(16, 256),
            feat_all,
            att_all,
            block_all,
            w_out,
        ),
        shape((RING, 8, 1024), F32),
        [pltpu.VMEM((1024, 896), BF16)],
    )
    total = call(
        reduce_kernel,
        (part.astype(BF16),),
        shape((8, 1024), F32),
        [pltpu.VMEM((RING, 8, 1024), BF16), dma(RING), dma(RING)],
        5,
    )
    weight_grads = total.reshape(8, 32, 32)[:, :31, :]
    features_grad = feat_grad.reshape(2, COLS, 256).transpose(1, 0, 2)[:, None]
    return features_grad, weight_grads


def solution(mesh):
    token = P("azim", "sweep", "beam", None)
    in_specs = (token, token) + (P(),) * 6
    out_specs = (token, P("azim", None, ("beam", "sweep")))
    return jax.shard_map(
        per_device, mesh=mesh, in_specs=in_specs, out_specs=out_specs, check_vma=False
    )
```

time: 756 us -> 136 us (0.18); the launches traced: 747 us -> 135 us
  waiting for transfers between devices: 466 us -> 0 us
  local copies, waits for them, and re-layouts: 185 us -> 9.37 us
  Pallas kernels: 0 us -> 122 us
  matrix products: 57.8 us -> 0 us
  other arithmetic: 17.5 us -> 2.7 us
  between operations: 14.4 us -> 0.68 us
    reduce_scatter x2 -> x0, waiting for transfers between devices: 295 us -> none  [the longest x1 150 us: per_device(): lax.psum_scatter(jnp.concatenate([projection_terms, conv_terms], axis=1),...]
    all_gather x2 -> x0, waiting for transfers between devices: 139 us -> none  [the longest x1 72 us: per_device(): lax.all_gather(key_proj, 'azim', axis=0, tiled=True)]
    pallas_call x0 -> x9, Pallas kernels: none -> 122 us  [call(): pl.pallas_call(kernel, out_shape=outputs, in_specs=[VMEM] * len(inputs),...]
    dot_general x21 -> x0, matrix products: 57.8 us -> none  [the longest x1 8.22 us: key_side(): jnp.einsum('sbhak,asbhe->ksbhe', weights_full.astype(jnp.bfloat16), split...]
    unnamed x129 -> x2, local copies, waits for them, and re-layouts: 51.9 us -> 2.2 us
    slice x33 -> x0, local copies, waits for them, and re-layouts: 46.4 us -> none  [the longest x29 42.1 us: gather_taps(): padded[first_at:first_at + col_count, second_at:second_at + sweeps, third...]
    another operation x35 -> x1, local copies, waits for them, and re-layouts: 41.8 us -> 0.7 us  [per_device(): edges = jnp.stack([cotangent[0, 0], cotangent[COLS - 1, 0]])]
    unnamed x6 -> x0, waiting for transfers between devices: 25 us -> none
  transfers between devices with their start and end apart: 11 -> 0, of which waited for: 10 -> 0; matrix products, arithmetic and copies ran while one was open for 6% -> 0% of each run, Pallas kernels for 0% -> 0%
where the time goes in v1:
time: 136 us; the launch traced here: 135 us
  Pallas kernels  122 us (90%)
  local copies, waits for them, and re-layouts  9.37 us (7%)
  other arithmetic  2.7 us (2%)
    pallas_call x9, Pallas kernels, call(): pl.pallas_call(kernel, out_shape=outputs, in_specs=[VMEM] * len(inputs),...  122 us

profile of v1, /device:TPU:1, one launch (start us, length us, event | category | flops | bytes accessed | tf_op | source)
XLA Modules:
  0.0 135.1 jit_solution(1718223682944375085)
XLA Ops:
  0.6 0.7 slice_bitcast_fusion.1
  1.3 0.6 pad_maximum_fusion.edges
  1.9 1.5 %copy.11 = bf16[2,64,256]{2,1,0:T(8,128)(2,1)} copy(bf16[2,64,256]{2,0,1:T(2,128)(2,1)} %bitcast.34) | data formatting | bytes 131072 | tf_op jit(solution)/shard_map/transpose | solution.py:531
  3.4 1.5 %copy.18 = bf16[64,1,2,256]{3,0,2,1:T(8,128)(2,1)} copy(bf16[64,1,2,256]{3,2,1,0:T(2,128)(2,1)} %param.9) | data formatting | bytes 131072 | tf_op args[1]
  4.9 16.5 %shard_map.95 = (bf16[8,2,64,256]{3,2,1,0:T(8,128)(2,1)}, bf16[8,2,256]{2,1,0:T(2,128)(2,1)}, bf16[8,2,256]{2,1,0:T(2,128)(2,1)}) custom-call(bf16[2,64,256]{2,1,0:T(8,128)(2,1)} %bitcast.33, bf16[2,2,256]{2,1,0:T(2,128)(2,1)} %pad_maximum_fusion.edges), custom_call_target="tpu_custom_call" | custom-call | tf_op jit(solution)/shard_map/pallas_call | solution.py:512
  21.4 1.3 reshape.45.low
  22.7 1.3 reshape.46.high
  24.0 5.4 %shard_map.96 = (f32[128,256]{1,0:T(8,128)}, bf16[16,64,128]{2,1,0:T(8,128)(2,1)}) custom-call(bf16[8,2,64,256]{3,2,1,0:T(8,128)(2,1)} %get-tuple-element.19.cot_all, bf16[8,2,256]{2,1,0:T(2,128)(2,1)} %get-tuple-element.20.low, bf16[8,2,256]{2,1,0:T(2,128)(2,1)} %get-tuple-element.21.high, bf16[128,256]{1,0:T(8,128)(2,1)} %bitcast.26, ...), custom_call_target="tpu_custom_call" | custom-call | tf_op jit(solution)/shard_map/pallas_call | solution.py:512
  29.4 21.5 %shard_map.97 = (bf16[16,64,128]{2,1,0:T(8,128)(2,1)}, bf16[16,64,128]{2,1,0:T(8,128)(2,1)}, bf16[8,128,256]{2,1,0:T(8,128)(2,1)}) custom-call(bf16[16,64,128]{2,1,0:T(8,128)(2,1)} %get-tuple-element.22.pack, bf16[128,256]{1,0:T(8,128)(2,1)} %bitcast.27), custom_call_target="tpu_custom_call" | custom-call | tf_op jit(solution)/shard_map/pallas_call | solution.py:512
  50.9 13.0 %shard_map.98 = (bf16[1024,128]{1,0:T(8,128)(2,1)}, bf16[1024,128]{1,0:T(8,128)(2,1)}) custom-call(bf16[1024,128]{1,0:T(8,128)(2,1)} %bitcast.29, bf16[1024,128]{1,0:T(8,128)(2,1)} %bitcast.30, s32[32,32]{1,0:T(8,128)} %mask.1), custom_call_target="tpu_custom_call" | custom-call | tf_op jit(solution)/shard_map/pallas_call | solution.py:512
  63.9 21.7 %shard_map.99 = (bf16[16,64,128]{2,1,0:T(8,128)(2,1)}, bf16[16,64,128]{2,1,0:T(8,128)(2,1)}) custom-call(bf16[16,64,128]{2,1,0:T(8,128)(2,1)} %bitcast.31, bf16[16,64,128]{2,1,0:T(8,128)(2,1)} %bitcast.32), custom_call_target="tpu_custom_call" | custom-call | tf_op jit(solution)/shard_map/pallas_call | solution.py:512
  85.6 2.9 %shard_map.100 = (bf16[128,256]{1,0:T(8,128)(2,1)}, bf16[128,256]{1,0:T(8,128)(2,1)}, bf16[8,128,128]{2,1,0:T(8,128)(2,1)}) custom-call(bf16[16,64,128]{2,1,0:T(8,128)(2,1)} %get-tuple-element.27.from_same, bf16[16,64,128]{2,1,0:T(8,128)(2,1)} %get-tuple-element.28.from_other, f32[128,256]{1,0:T(8,128)} %get-tuple-element.29.grad, bf16[256,256]{1,0:T(8,128)(2,1)} %w_query.3, ...), custom_call_target="tpu_custom_call" | custom-call | tf_op jit(solution)/shard_map/pallas_call | solution.py:512
  88.5 1.5 %copy.17 = bf16[2,64,256]{2,0,1:T(2,128)(2,1)} copy(bf16[2,64,256]{2,1,0:T(8,128)(2,1)} %bitcast.36) | data formatting | bytes 131072 | tf_op jit(solution)/shard_map/reshape | solution.py:611
  90.0 14.0 %shard_map.101 = (bf16[8,128,256]{2,1,0:T(8,128)(2,1)}, bf16[8,128,128]{2,1,0:T(8,128)(2,1)}) custom-call(bf16[128,256]{1,0:T(8,128)(2,1)} %get-tuple-element.32.att, bf16[8,128,128]{2,1,0:T(8,128)(2,1)} %get-tuple-element.33.blocks), custom_call_target="tpu_custom_call" | custom-call | tf_op jit(solution)/shard_map/pallas_call | solution.py:512
  104.0 4.2 %shard_map.102 = f32[32,8,1024]{2,1,0:T(8,128)} custom-call(bf16[8,2,64,256]{3,2,1,0:T(8,128)(2,1)} %get-tuple-element.19.cot_all, bf16[16,256]{1,0:T(8,128)(2,1)} %reshape.45.low, bf16[16,256]{1,0:T(8,128)(2,1)} %reshape.46.high, bf16[8,128,256]{2,1,0:T(8,128)(2,1)} %get-tuple-element.31.feat_all, bf16[8,128,256]{2,1,0:T(8,128)(2,1)} %get-tuple-element.34.att_all, ...), custom_call_target="tpu_custom_call" | custom-call | tf_op jit(solution)/shard_map/pallas_call | solution.py:512
  108.2 2.1 %convert_element_type.3.part = bf16[32,8,1024]{2,1,0:T(8,128)(2,1)} convert(f32[32,8,1024]{2,1,0:T(8,128)} %shard_map.102) | non-fusion elementwise | flops 262144 | bytes 1572864 | tf_op jit(solution)/shard_map/convert_element_type | solution.py:605
  110.3 23.2 %shard_map.103 = f32[8,1024]{1,0:T(8,128)} custom-call(bf16[32,8,1024]{2,1,0:T(8,128)(2,1)} %convert_element_type.3.part), custom_call_target="tpu_custom_call" | custom-call | tf_op jit(solution)/shard_map/pallas_call | solution.py:512
  133.5 0.9 reshape.47
  134.3 0.7 copy.14

commit v2 on v0

v2 whole, which is shorter than its diff:
```python
import jax
import jax.numpy as jnp
from jax import lax
from jax.experimental import pallas as pl
from jax.experimental.pallas import tpu as pltpu
from jax.sharding import PartitionSpec as P

HEADS = 8
HEAD = 32
COLS = 64
RING = 32
CHIPS = 16
GROUP = 8
SWEEPS = 4
TAPS = 27
TILE = 256
SCALE = HEAD ** (-0.5)
MASKED = -1e30
MESH = pl.DeviceIdType.MESH
VMEM = pl.BlockSpec(memory_space=pltpu.VMEM)
F32 = jnp.float32
BF16 = jnp.bfloat16


def place():
    return lax.axis_index("azim"), lax.axis_index("beam"), lax.axis_index("sweep")


def member(azim, index):
    return (azim, lax.div(index, SWEEPS), lax.rem(index, SWEEPS))


def remote(src, dst, send, recv, device):
    return pltpu.make_async_remote_copy(
        src_ref=src, dst_ref=dst, send_sem=send, recv_sem=recv, device_id=device, device_id_type=MESH
    )


def each(first, last, action):
    def step(i, carry):
        action(i)
        return carry

    lax.fori_loop(first, last, step, 0)


def shifted(block, low, high):
    rows = lax.broadcasted_iota(jnp.int32, block.shape, 0)
    down = jnp.where(rows == 0, low, pltpu.roll(block, 1, 0))
    up = jnp.where(rows == COLS - 1, high, pltpu.roll(block, COLS - 1, 0))
    return up, block, down


def regroup():
    col = lax.broadcasted_iota(jnp.int32, (1, 1024), 1)
    source = ((col >> 5) & 3) * 256 + (col >> 7) * 32 + (col & 31)
    row = lax.broadcasted_iota(jnp.int32, (1024, 1024), 0)
    return jnp.where(row == source, 1.0, 0.0).astype(BF16)


def dot(left, right):
    return jnp.dot(left, right, preferred_element_type=F32)


def dot_nt(left, right):
    return lax.dot_general(left, right, (((1,), (1,)), ((), ())), preferred_element_type=F32)


def split_beams(block):
    wide = block[...].astype(F32)
    return jnp.concatenate([wide[:, 0, :], wide[:, 1, :]], axis=0)


class Route:
    def __init__(self):
        self.azim, self.beam, self.sweep = place()
        self.me = self.beam * SWEEPS + self.sweep
        self.chip = lax.div(self.azim, 2)
        self.core = lax.rem(self.azim, 2)
        self.sibling = (2 * self.chip + 1 - self.core, self.beam, self.sweep)
        self.after = lax.rem(self.azim + 1, RING)
        self.before = lax.rem(self.azim + RING - 1, RING)

    def ring(self, i):
        return (lax.rem(self.azim + i, RING), self.beam, self.sweep)

    def target(self, i):
        return lax.rem(self.chip + i, CHIPS)

    def like(self, q):
        return (2 * q + self.core, self.beam, self.sweep)

    def peer(self, i):
        return lax.rem(self.me + i, GROUP)

    def mate(self, index):
        return member(self.azim, index)

    def beside(self, d, other):
        beam = 1 - self.beam if other else self.beam
        return (self.azim, beam, lax.rem(self.sweep + d + SWEEPS, SWEEPS))


def greet_all(r):
    barrier = pltpu.get_barrier_semaphore()

    def tell(device):
        pl.semaphore_signal(barrier, inc=1, device_id=device, device_id_type=MESH)

    each(1, RING, lambda i: tell(r.ring(i)))
    each(1, GROUP, lambda i: tell(member(r.after, r.peer(i))))
    each(1, GROUP, lambda i: tell(member(r.before, r.peer(i))))
    each(1, GROUP, lambda i: tell(r.mate(r.peer(i))))
    return barrier, RING - 1 + 3 * (GROUP - 1)


def edge_copies(r, cot, low, high, sems):
    def up(i, slot):
        return remote(cot.at[COLS - 1], low.at[slot], sems.at[0, i], sems.at[1, slot], member(r.after, i))

    def down(i, slot):
        return remote(cot.at[0], high.at[slot], sems.at[2, i], sems.at[3, slot], member(r.before, i))

    return up, down


def near_copies(r, cot_own, near, near_half, sems):
    copies = []
    for slot, d in ((0, 1), (1, -1)):
        copies.append(remote(cot_own, near.at[slot], sems.at[0, slot], sems.at[1, slot], r.beside(d, False)))
    for d in (-1, 0, 1):
        copies.append(
            remote(
                cot_own.at[1 - r.beam],
                near_half.at[1 - d],
                sems.at[0, 3 - d],
                sems.at[1, 3 - d],
                r.beside(d, True),
            )
        )
    return copies


def grad_of_layer(r, own, near, near_half, low, high, conv):
    total = own
    for j in (-1, 0, 1):
        for k in (-1, 0, 1):
            ups, mids, downs = [], [], []
            for mine in (0, 1):
                s_at = r.sweep - j
                inside = (s_at >= 0) & (s_at < SWEEPS)
                if mine - k == -1:
                    inside = inside & (r.beam == 1)
                    block = near_half[1 - j]
                elif mine - k == 2:
                    inside = inside & (r.beam == 0)
                    block = near_half[1 - j]
                elif j == 0:
                    block = own[(mine - k) * COLS : (mine - k + 1) * COLS]
                else:
                    block = near[0 if j == 1 else 1, mine - k]
                s_at = jnp.clip(s_at, 0, SWEEPS - 1)
                index = jnp.clip(r.beam + (mine - k) // 2, 0, 1) * SWEEPS + s_at
                half = (mine - k) % 2
                keep = jnp.where(inside, 1.0, 0.0)
                up, mid, down = shifted(
                    block.astype(F32) * keep,
                    low[index].astype(F32)[half : half + 1] * keep,
                    high[index].astype(F32)[half : half + 1] * keep,
                )
                ups.append(up)
                mids.append(mid)
                downs.append(down)
            for i, rows in ((-1, ups), (0, mids), (1, downs)):
                tap = 9 * (i + 1) + 3 * (j + 1) + (k + 1)
                total += dot_nt(jnp.concatenate(rows, axis=0).astype(BF16), conv[tap])
    return total


def attend(core, same, other, mask, cols_all, cols_own, allowed, back, keys_sum):
    sub = lax.broadcasted_iota(jnp.int32, (32, 32), 0)
    lane = lax.broadcasted_iota(jnp.int32, (32, 32), 1)
    key_sector = jnp.where(sub < CHIPS, 2 * sub + core, 2 * (sub - CHIPS) + 1 - core)
    key_hot = jnp.where(lane == key_sector, 1.0, 0.0).astype(BF16)
    by_query = dot_nt(key_hot, mask[...].astype(F32).astype(BF16)).astype(BF16)
    lane = lax.broadcasted_iota(jnp.int32, (32, 1024), 1)
    sub = lax.broadcasted_iota(jnp.int32, (32, 1024), 0)
    query_hot = jnp.where(sub == 2 * (lane >> 6) + core, 1.0, 0.0).astype(BF16)
    full = dot(by_query, query_hot)
    own = same[...].reshape(1024, 128)
    own_t = own.astype(F32).T.astype(BF16)
    cols_all[:, 0:1024] = own_t
    cols_all[:, 1024:2048] = other[...].reshape(1024, 128).astype(F32).T.astype(BF16)
    for t in range(1024 // TILE):
        cols_own[t] = own_t[:, t * TILE : (t + 1) * TILE]
        allowed[t] = full[:, t * TILE : (t + 1) * TILE]
    keys_sum[...] = jnp.zeros_like(keys_sum)

    def tile(t, carry):
        cols = cols_own[t]
        rows = same[pl.ds(t * (TILE // COLS), TILE // COLS)].reshape(TILE, 128)
        rows_all = jnp.concatenate([same[...], other[...]], axis=0).reshape(2048, 128)
        keep = allowed[t][:, None, :]
        blank = jnp.zeros((96, TILE), BF16)
        score = dot(rows_all, jnp.concatenate([cols[32:64], blank], axis=0))
        score = score.reshape(32, COLS, TILE) * SCALE
        score = jnp.where(keep > 0.5, score, MASKED)
        peak = jnp.max(jnp.max(score, axis=0), axis=0, keepdims=True)
        weight = jnp.exp(score - peak[None])
        total = jnp.sum(jnp.sum(weight, axis=0), axis=0, keepdims=True)
        weight = weight * (keep * (1.0 / total)[None])
        probs = weight.reshape(2048, TILE).astype(BF16)
        attended = dot(cols_all[96:128, :], probs).astype(BF16)
        grad_att = cols[64:96]
        delta = jnp.sum(grad_att.astype(F32) * attended.astype(F32), axis=0, keepdims=True)
        grad_prob = dot(rows_all, jnp.concatenate([blank, grad_att], axis=0))
        grad_score = weight * (grad_prob.reshape(32, COLS, TILE) - delta[None])
        grad_score = grad_score.reshape(2048, TILE).astype(BF16)
        grad_query = dot(cols_all[0:32, :], grad_score) * SCALE
        place_at = lax.broadcasted_iota(jnp.int32, (TILE, 128), 1) >> 5
        zero = jnp.zeros((TILE, 128), BF16)
        keys_sum[...] += (
            dot(grad_score, jnp.where(place_at == 1, rows, zero)) * SCALE
            + dot(probs, jnp.where(place_at == 2, rows, zero))
        ).reshape(2, 1024, 128)
        joined = jnp.concatenate(
            [grad_query, jnp.zeros((64, TILE), F32), attended.astype(F32)], axis=0
        )
        back[pl.ds(pl.multiple_of(t * TILE, TILE), TILE), :] = joined.T
        return carry

    lax.fori_loop(0, 1024 // TILE, tile, 0)


def fill_taps(me, cot_all, low, high, taps):
    row = lax.broadcasted_iota(jnp.int32, (256, 128), 0)
    col = lax.broadcasted_iota(jnp.int32, (256, 128), 1)
    pick = jnp.where(row == me * HEAD + (col & 31), 1.0, 0.0).astype(BF16)
    own = dot(cot_all[...].reshape(1024, 256), pick)

    def flat(ref):
        wide = ref[...].astype(F32)
        return dot(wide.reshape(16, 256).astype(BF16), pick)

    own_low = flat(low)
    own_high = flat(high)
    moved = []
    for n in range(16):
        moved.append(
            shifted(own[n * COLS : (n + 1) * COLS], own_low[n : n + 1], own_high[n : n + 1])
        )
    lane = lax.broadcasted_iota(jnp.int32, (COLS, 128), 1) >> 5
    zero = jnp.zeros((COLS, 128), F32)

    def find(n, tap):
        if tap >= TAPS:
            return zero
        i, j, k = tap // 9, tap // 3 % 3 - 1, tap % 3 - 1
        s = (n // 2) % SWEEPS - j
        b = (n // 2) // SWEEPS * 2 + n % 2 - k
        if not (0 <= s < SWEEPS and 0 <= b < 4):
            return zero
        return moved[(b // 2 * SWEEPS + s) * 2 + b % 2][i]

    for g in range(7):
        for n in range(16):
            value = find(n, 4 * g)
            for r in (1, 2, 3):
                value = jnp.where(lane == r, find(n, 4 * g + r), value)
            taps[n * COLS : (n + 1) * COLS, g * 128 : (g + 1) * 128] = value.astype(BF16)


def whole_kernel(
    features,
    cotangent,
    w_query,
    w_key,
    w_value,
    w_out,
    w_conv,
    mask,
    feat_grad,
    total,
    conv,
    feat,
    cot_own,
    near,
    near_half,
    low,
    high,
    cot_all,
    feat_all,
    order,
    pack,
    same,
    other,
    cols_all,
    cols_own,
    allowed,
    back,
    keys_sum,
    keys_in,
    out_same,
    from_same,
    grad_keep,
    att,
    blocks,
    att_all,
    block_all,
    taps,
    part,
    part_in,
    merged,
    landed,
    conv_sem,
    edge_sem,
    near_sem,
    cot_sem,
    feat_sem,
    pack_sem,
    pair_sem,
    keys_sem,
    back_sem,
    att_sem,
    block_sem,
    part_sem,
    sum_sem,
):
    r = Route()
    load = pltpu.make_async_copy(w_conv, conv, conv_sem)
    load.start()
    barrier, expected = greet_all(r)
    order[...] = regroup()
    feat[...] = split_beams(features).astype(BF16)
    own = split_beams(cotangent)
    cot_own[...] = own.astype(BF16).reshape(2, COLS, 256)
    rows = feat[...]
    queries = dot(rows, w_query[...]).astype(BF16)
    keys = dot(rows, w_key[...]).astype(BF16)
    values = dot(rows, w_value[...]).astype(BF16)
    feat_all[pl.ds(r.me, 1)] = rows[None]
    cot_all[pl.ds(r.me, 1)] = cot_own[...][None]
    pl.semaphore_wait(barrier, expected)

    up, down = edge_copies(r, cotangent, low, high, edge_sem)
    near_all = near_copies(r, cot_own, near, near_half, near_sem)
    each(0, GROUP, lambda i: up(i, r.me).start())
    each(0, GROUP, lambda i: down(i, r.me).start())
    for copy in near_all:
        copy.start()
    load.wait()
    each(0, GROUP, lambda i: up(i, i).wait())
    each(0, GROUP, lambda i: down(i, i).wait())
    for copy in near_all:
        copy.wait()
    grad = grad_of_layer(r, own, near, near_half, low, high, conv)
    grad_keep[...] = grad
    grad_att = dot_nt(grad.astype(BF16), w_out[...]).astype(BF16)
    wide = jnp.concatenate([keys, queries, grad_att, values], axis=1)
    packed = dot(wide, order[...]).astype(BF16)
    for b in (0, 1):
        for h in range(HEADS):
            pack[b * HEADS + h] = packed[b * COLS : (b + 1) * COLS, h * 128 : (h + 1) * 128]

    def head_copy(i, slot):
        return remote(
            pack.at[r.target(i)],
            same.at[slot],
            pack_sem.at[0, r.target(i)],
            pack_sem.at[1, slot],
            r.like(r.target(i)),
        )

    def relay(q):
        return remote(same.at[q], other.at[q], pair_sem.at[0, q], pair_sem.at[1, q], r.sibling)

    def cot_copy(i, slot):
        return remote(
            cot_own, cot_all.at[slot], cot_sem.at[0, r.peer(i)], cot_sem.at[1, slot], r.mate(r.peer(i))
        )

    def feat_copy(i, slot):
        return remote(
            feat, feat_all.at[slot], feat_sem.at[0, r.peer(i)], feat_sem.at[1, slot], r.mate(r.peer(i))
        )

    each(1, CHIPS, lambda i: head_copy(i, r.chip).start())
    keep = pltpu.make_async_copy(pack.at[r.chip], same.at[r.chip], conv_sem)
    keep.start()
    each(1, GROUP, lambda i: cot_copy(i, r.me).start())
    each(1, GROUP, lambda i: feat_copy(i, r.me).start())
    keep.wait()
    relay(r.chip).start()

    def pass_on(i):
        head_copy(i, r.target(i)).wait()
        relay(r.target(i)).start()

    each(1, CHIPS, pass_on)
    each(0, CHIPS, lambda q: relay(q).wait())

    attend(r.core, same, other, mask, cols_all, cols_own, allowed, back, keys_sum)

    swap = remote(keys_sum.at[1], keys_in, keys_sem.at[0], keys_sem.at[1], r.sibling)
    swap.start()
    swap.wait()
    out_same[...] = (keys_sum[0] + back[...] + keys_in[...]).astype(BF16).reshape(CHIPS, COLS, 128)

    def back_copy(i, slot):
        return remote(
            out_same.at[r.target(i)],
            from_same.at[slot],
            back_sem.at[0, r.target(i)],
            back_sem.at[1, slot],
            r.like(r.target(i)),
        )

    each(1, CHIPS, lambda i: back_copy(i, r.chip).start())
    from_same[pl.ds(r.chip, 1)] = out_same[pl.ds(r.chip, 1)]
    each(1, GROUP, lambda i: cot_copy(i, r.peer(i)).wait())
    each(1, GROUP, lambda i: feat_copy(i, r.peer(i)).wait())
    fill_taps(r.me, cot_all, low, high, taps)
    each(1, CHIPS, lambda i: back_copy(i, r.target(i)).wait())

    packed = jnp.concatenate(
        [
            jnp.concatenate([from_same[b * HEADS + h] for h in range(HEADS)], axis=1)
            for b in (0, 1)
        ],
        axis=0,
    )
    grad = grad_keep[...]
    last = dot(grad.astype(BF16), order[768:1024, :])
    group = (lax.broadcasted_iota(jnp.int32, (2 * COLS, 1024), 1) >> 5) & 3
    mixed = jnp.where(group == 3, last, packed.astype(F32)).astype(BF16)
    for h in range(HEADS):
        blocks[h] = mixed[:, h * 128 : (h + 1) * 128]
    wide = dot_nt(packed, order[...]).astype(BF16)
    att[...] = wide[:, 768:1024]

    def att_copy(i, slot):
        return remote(
            att, att_all.at[slot], att_sem.at[0, r.peer(i)], att_sem.at[1, slot], r.mate(r.peer(i))
        )

    def block_copy(i, slot):
        return remote(
            blocks.at[r.peer(i)],
            block_all.at[slot],
            block_sem.at[0, r.peer(i)],
            block_sem.at[1, slot],
            r.mate(r.peer(i)),
        )

    each(1, GROUP, lambda i: att_copy(i, r.me).start())
    each(1, GROUP, lambda i: block_copy(i, r.me).start())
    att_all[pl.ds(r.me, 1)] = wide[:, 768:1024][None]
    block_all[pl.ds(r.me, 1)] = blocks[pl.ds(r.me, 1)]
    feat_grad[...] = (
        grad
        + dot_nt(wide[:, 0:256], w_query[...])
        + dot_nt(wide[:, 256:512], w_key[...])
        + dot_nt(wide[:, 512:768], w_value[...])
    ).astype(BF16)
    feats = feat_all[...].reshape(1024, 256)
    feats_t = feats.astype(F32).T.astype(BF16)
    each(1, GROUP, lambda i: att_copy(i, r.peer(i)).wait())
    each(1, GROUP, lambda i: block_copy(i, r.peer(i)).wait())

    atts = att_all[...].reshape(1024, 256)
    layer = feats.astype(F32) + dot(atts, w_out[...])
    shares = block_all[...].reshape(1024, 128)
    first = dot(feats_t, shares)
    fourth = dot(atts.astype(F32).T.astype(BF16), shares)
    col = lax.broadcasted_iota(jnp.int32, (256, 128), 1) >> 5
    first = jnp.where(col == 3, fourth, first).reshape(CHIPS, 2, 8, 128)
    rest = dot(layer.T.astype(BF16), taps[...]).reshape(CHIPS, 2, 8, 896)
    for c in (0, 1):
        part[c, :, :, 0:128] = first[:, c]
        part[c, :, :, 128:1024] = rest[:, c]

    pair = remote(part.at[1 - r.core], part_in, part_sem.at[0], part_sem.at[1], r.sibling)
    pair.start()
    pair.wait()
    merged[...] = (part[r.core] + part_in[...]).astype(BF16)

    def sum_copy(i, slot):
        return remote(
            merged.at[r.target(i)],
            landed.at[slot],
            sum_sem.at[0, r.target(i)],
            sum_sem.at[1, slot],
            r.like(r.target(i)),
        )

    each(1, CHIPS, lambda i: sum_copy(i, r.chip).start())
    total[...] = merged[r.chip].astype(F32)

    def add(i):
        sum_copy(i, r.target(i)).wait()
        total[...] += landed[r.target(i)].astype(F32)

    each(1, CHIPS, add)


def shape(dims, kind=BF16):
    return jax.ShapeDtypeStruct(dims, kind)


def dma(*dims):
    return pltpu.SemaphoreType.DMA(dims)


def per_device(features, cotangent, w_query, w_key, w_value, w_out, w_conv, sector_mask):
    anywhere = pl.BlockSpec(memory_space=pl.ANY)
    vmem = pltpu.VMEM
    heads = (CHIPS, COLS, 128)
    feat_grad, total = pl.pallas_call(
        whole_kernel,
        out_shape=(shape((2 * COLS, 256)), shape((8, 1024), F32)),
        in_specs=[VMEM] * 6 + [anywhere, VMEM],
        out_specs=(VMEM, VMEM),
        scratch_shapes=[
            vmem((TAPS, 256, 256), BF16),
            vmem((2 * COLS, 256), BF16),
            vmem((2, COLS, 256), BF16),
            vmem((2, 2, COLS, 256), BF16),
            vmem((3, COLS, 256), BF16),
            vmem((GROUP, 2, 256), BF16),
            vmem((GROUP, 2, 256), BF16),
            vmem((GROUP, 2, COLS, 256), BF16),
            vmem((GROUP, 2 * COLS, 256), BF16),
            vmem((1024, 1024), BF16),
            vmem(heads, BF16),
            vmem(heads, BF16),
            vmem(heads, BF16),
            vmem((128, 2048), BF16),
            vmem((1024 // TILE, 128, TILE), BF16),
            vmem((1024 // TILE, 32, TILE), F32),
            vmem((1024, 128), F32),
            vmem((2, 1024, 128), F32),
            vmem((1024, 128), F32),
            vmem(heads, BF16),
            vmem(heads, BF16),
            vmem((2 * COLS, 256), F32),
            vmem((2 * COLS, 256), BF16),
            vmem((HEADS, 2 * COLS, 128), BF16),
            vmem((GROUP, 2 * COLS, 256), BF16),
            vmem((GROUP, 2 * COLS, 128), BF16),
            vmem((1024, 896), BF16),
            vmem((2, CHIPS, 8, 1024), F32),
            vmem((CHIPS, 8, 1024), F32),
            vmem((CHIPS, 8, 1024), BF16),
            vmem((CHIPS, 8, 1024), BF16),
            pltpu.SemaphoreType.DMA,
            dma(4, GROUP),
            dma(2, 5),
            dma(2, GROUP),
            dma(2, GROUP),
            dma(2, CHIPS),
            dma(2, CHIPS),
            dma(2),
            dma(2, CHIPS),
            dma(2, GROUP),
            dma(2, GROUP),
            dma(2),
            dma(2, CHIPS),
        ],
        compiler_params=pltpu.CompilerParams(
            collective_id=1, has_side_effects=True, vmem_limit_bytes=62 * 1024 * 1024
        ),
    )(
        features.reshape(COLS, 2, 256),
        cotangent.reshape(COLS, 2, 256),
        w_query,
        w_key,
        w_value,
        w_out,
        w_conv.transpose(1, 0, 2),
        sector_mask,
    )
    weight_grads = total.reshape(8, 32, 32)[:, :31, :]
    features_grad = feat_grad.reshape(2, COLS, 256).transpose(1, 0, 2)[:, None]
    return features_grad, weight_grads


def solution(mesh):
    token = P("azim", "sweep", "beam", None)
    in_specs = (token, token) + (P(),) * 6
    out_specs = (token, P("azim", None, ("beam", "sweep")))
    return jax.shard_map(
        per_device, mesh=mesh, in_specs=in_specs, out_specs=out_specs, check_vma=False
    )
```

time: 756 us -> 87.7 us (0.12); the launches traced: 747 us -> 87.3 us
  waiting for transfers between devices: 466 us -> 0 us
  local copies, waits for them, and re-layouts: 185 us -> 3.11 us
  Pallas kernels: 0 us -> 83.6 us
  matrix products: 57.8 us -> 0 us
  other arithmetic: 17.5 us -> 0 us
  between operations: 14.4 us -> 0.64 us
    reduce_scatter x2 -> x0, waiting for transfers between devices: 295 us -> none  [the longest x1 150 us: per_device(): lax.psum_scatter(jnp.concatenate([projection_terms, conv_terms], axis=1),...]
    all_gather x2 -> x0, waiting for transfers between devices: 139 us -> none  [the longest x1 72 us: per_device(): lax.all_gather(key_proj, 'azim', axis=0, tiled=True)]
    pallas_call x0 -> x1, Pallas kernels: none -> 83.6 us  [per_device(): pl.pallas_call(whole_kernel, out_shape=(shape((2 * COLS, 256)), shape((8,...]
    dot_general x21 -> x0, matrix products: 57.8 us -> none  [the longest x1 8.22 us: key_side(): jnp.einsum('sbhak,asbhe->ksbhe', weights_full.astype(jnp.bfloat16), split...]
    unnamed x129 -> x1, local copies, waits for them, and re-layouts: 51.9 us -> 0.73 us
    slice x33 -> x0, local copies, waits for them, and re-layouts: 46.4 us -> none  [the longest x29 42.1 us: gather_taps(): padded[first_at:first_at + col_count, second_at:second_at + sweeps, third...]
    another operation x35 -> x0, local copies, waits for them, and re-layouts: 41.8 us -> none  [the longest x29 41 us: gather_taps(): return jnp.stack(pieces, axis=3)]
    unnamed x6 -> x0, waiting for transfers between devices: 25 us -> none
  transfers between devices with their start and end apart: 11 -> 0, of which waited for: 10 -> 0; matrix products, arithmetic and copies ran while one was open for 6% -> 0% of each run, Pallas kernels for 0% -> 0%
where the time goes in v2:
time: 87.7 us; the launch traced here: 87.3 us
  Pallas kernels  83.6 us (95%)
  local copies, waits for them, and re-layouts  3.11 us (4%)
    pallas_call x1, Pallas kernels, per_device(): pl.pallas_call(whole_kernel, out_shape=(shape((2 * COLS, 256)), shape((8,...  83.6 us

profile of v2, /device:TPU:1, one launch (start us, length us, event | category | flops | bytes accessed | tf_op | source)
XLA Modules:
  0.0 87.3 jit_solution(5975848790788643004)
XLA Ops:
  0.6 83.6 %shard_map.95 = (bf16[128,256]{1,0:T(8,128)(2,1)}, f32[8,1024]{1,0:T(8,128)}) custom-call(bf16[64,2,256]{2,1,0:T(2,128)(2,1)} %bitcast.12, bf16[64,2,256]{2,1,0:T(2,128)(2,1)} %bitcast.13, bf16[256,256]{1,0:T(8,128)(2,1)} %w_query.1, bf16[256,256]{1,0:T(8,128)(2,1)} %w_key.1, bf16[256,256]{1,0:T(8,128)(2,1)} %w_value.1, bf16[256,256]{1,0:T(8,128)(2,1)} %w_out.1, ...), custom_call_target="tpu_custom_call" | custom-call | tf_op jit(solution)/shard_map/pallas_call | solution.py:518
  84.2 1.5 %copy.14 = bf16[2,64,256]{2,0,1:T(2,128)(2,1)} copy(bf16[2,64,256]{2,1,0:T(8,128)(2,1)} %bitcast.15) | data formatting | bytes 131072 | tf_op jit(solution)/shard_map/reshape | solution.py:583
  85.8 0.8 reshape.19
  86.6 0.7 copy.12
